TPU v7x, 32 devices: a whole 2x2x4 slice. The times are simulated.
32 devices in a mesh: row: 4 (over y, x), col: 8 (over z, core).
Axes of the slice: x: 2, y: 2, z: 4, core: 2. Of those that a mesh axis runs over, the one named last changes fastest.
Arguments:
- tokens: bfloat16 [1024, 53248], P(('row', 'col')), may hold values from -6 to 6
- eigvecs: float32 [53248, 2048], P('row', 'col'), may hold values from -0.02734375 to 0.02734375
- eigvals: float32 [2048], P('col'), may hold values from 0.25 to 4
- v_first: float32 [53248, 256], P(('row', 'col')), may hold values from -0.109375 to 0.109375
- v_second: float32 [53248, 256], P(('row', 'col')), may hold values from -0.109375 to 0.109375
- t_first: float32 [256, 256], replicated, may hold values from -0.375 to 0.375
- t_second: float32 [256, 256], replicated, may hold values from -0.375 to 0.375
Outputs:
- whitened: float32 [1024, 2048], P('row', 'col')
All inputs are finite; a program needn't handle non-finite values.
Results may differ from a plain program's by a relative error of at most 0.0029.
Values may be sent and summed in bfloat16 or wider, within the bound.
No kernel may reach another device: no remote copies, remote signals or barrier semaphores. Data moves between devices by JAX's collectives and lax.ppermute only.
A program may use at most 128 MiB of HBM per device.

v0:
```python
import jax
import jax.numpy as jnp
from jax import lax
from jax.sharding import PartitionSpec as P


def local_update(block, panel, factor, inner):
    middle = jnp.dot(
        factor, inner, precision=lax.Precision.HIGHEST, preferred_element_type=jnp.float32
    )
    return block - jnp.dot(
        panel, middle, precision=lax.Precision.HIGHEST, preferred_element_type=jnp.float32
    )


def partial_inner(panel, block):
    return jnp.dot(
        panel.T, block, precision=lax.Precision.HIGHEST, preferred_element_type=jnp.float32
    )


def per_device(tokens, eigvecs, eigvals, v_first, v_second, t_first, t_second):
    block = lax.all_to_all(eigvecs, "col", split_axis=0, concat_axis=1, tiled=True)
    for panel, factor in ((v_second, t_second), (v_first, t_first)):
        inner = lax.psum(partial_inner(panel, block), ("row", "col"))
        block = local_update(block, panel, factor, inner)
    every_value = lax.all_gather(eigvals, "col", axis=0, tiled=True)
    whitening = (block * lax.rsqrt(every_value)[None, :]).astype(jnp.bfloat16)
    slab = lax.all_to_all(tokens, ("row", "col"), split_axis=1, concat_axis=0, tiled=True)
    partial_value = jnp.dot(slab, whitening, preferred_element_type=jnp.float32)
    by_column = lax.psum_scatter(partial_value, "col", scatter_dimension=1, tiled=True)
    summed = lax.psum_scatter(by_column, "row", scatter_dimension=0, tiled=True)
    return summed


def solution(mesh):
    in_specs = (
        P(("row", "col"), None),
        P("row", "col"),
        P("col"),
        P(("row", "col"), None),
        P(("row", "col"), None),
        P(),
        P(),
    )
    out_specs = P("row", "col")
    return jax.shard_map(
        per_device, mesh=mesh, in_specs=in_specs, out_specs=out_specs, check_vma=False
    )
```

profile of v0, /device:TPU:0, one launch (start us, length us, event | category | flops | bytes accessed | tf_op | source)
XLA Modules:
  0.0 837.7 jit_solution(9575933095389601247)
XLA Ops:
  6.5 13.8 %copy.15 = f32[8,1664,256]{1,2,0:T(8,128)} copy(f32[8,1664,256]{2,1,0:T(8,128)} %bitcast.39) | data formatting | bytes 27262976 | tf_op jit(solution)/shard_map/all_to_all | solution.py:23
  20.4 6.4 all-to-all-start
  26.7 4.1 copy.20
  30.8 292.2 %all-to-all-done = f32[8,1664,256]{1,2,0:T(8,128)} async-done(((f32[8,1664,256]{1,2,0:T(8,128)}), f32[8,1664,256]{1,2,0:T(8,128)}, u32[]{:S(2)}, u32[]{:S(2)}) %all-to-all-start) | async-done | bytes 13631520 | tf_op jit(solution)/shard_map/all_to_all | solution.py:23
  323.0 4.1 all-to-all-start.1
  327.2 0.0 all-reduce.3.cloned.1.call-start
  327.2 25.8 %fusion.2 = f32[256,2048]{1,0:T(8,128)} fusion(f32[1664,256]{1,0:T(8,128)S(1)} %copy-done, f32[1664,2048]{0,1:T(8,128)} %bitcast.2), kind=kOutput, calls=%fused_computation.7 | convolution fusion | flops 10468982784 | bytes 17432576 | tf_op jit(solution)/shard_map/dot_general | solution.py:17
  353.1 0.2 all-reduce.5.cloned.1.call-start
  353.3 151.8 %all-reduce.3.cloned.1.call-done = f32[256,2048]{1,0:T(8,128)} async-done(((f32[256,2048]{1,0:T(8,128)}), f32[256,2048]{1,0:T(8,128)}) %all-reduce.3.cloned.1.call-update) | async-done | bytes 2097168 | tf_op jit(solution)/shard_map/psum | solution.py:25
  505.2 5.2 fusion.3
  510.3 16.9 %bitcast_subtract_fusion.1 = f32[1664,2048]{0,1:T(8,128)S(1)} fusion(f32[1664,2048]{0,1:T(8,128)} %bitcast.2, f32[2048,256]{1,0:T(8,128)S(1)} %fusion.3, f32[1664,256]{1,0:T(8,128)S(1)} %copy-done), kind=kOutput, calls=%fused_computation.3 | convolution fusion | flops 10472390656 | bytes 31064064 | tf_op jit(solution)/shard_map/dot_general | solution.py:11
  527.3 4.9 copy-done.2
  532.1 13.1 %convolution_bitcast_fusion.1 = f32[256,2048]{0,1:T(8,128)} fusion(f32[1664,2048]{0,1:T(8,128)S(1)} %bitcast_subtract_fusion.1, f32[1664,256]{1,0:T(8,128)S(1)} %copy-done.3), kind=kOutput, calls=%fused_computation.6 | convolution fusion | flops 10468982784 | bytes 17432576 | tf_op jit(solution)/shard_map/dot_general | solution.py:17
  545.3 0.0 reduce-scatter.3.cloned.1.call-start
  545.4 0.6 copy-done.6
  546.0 10.6 %all-gather = f32[8,1,256]{2,1,0:T(1,128)S(1)} all-gather(f32[1,1,256]{2,1,0:T(1,128)S(1)} %bitcast.43), channel_id=1, replica_groups=mesh['row'=4,'col'=8] {'col'}, dimensions={0}, use_global_device_ids=true | all-gather | bytes 9216 | tf_op jit(solution)/shard_map/all_gather | solution.py:27
  556.6 122.3 %all-reduce.5.cloned.1.call-done = f32[256,2048]{0,1:T(8,128)} async-done(((f32[256,2048]{0,1:T(8,128)}), f32[256,2048]{0,1:T(8,128)}) %all-reduce.5.cloned.1.call-update) | async-done | bytes 2097168 | tf_op jit(solution)/shard_map/psum | solution.py:25
  678.9 3.5 fusion.4
  682.4 16.4 %fusion.1 = bf16[1664,2048]{0,1:T(8,128)(2,1)} fusion(f32[1664,2048]{0,1:T(8,128)} %copy-done.2, f32[2048,256]{1,0:T(8,128)S(1)} %fusion.4, f32[1664,256]{1,0:T(8,128)S(1)} %copy-done.3, f32[2048]{0:T(1024)S(1)} %bitcast.42), kind=kOutput, calls=%fused_computation.2 | convolution fusion | flops 10479206400 | bytes 24256512 | tf_op jit(solution)/shard_map/dot_general | solution.py:11
  698.8 12.9 %convolution_bitcast_fusion = f32[1024,2048]{0,1:T(8,128)} fusion(bf16[1664,2048]{0,1:T(8,128)(2,1)} %fusion.1, bf16[1024,1664]{1,0:T(8,128)(2,1)} %bitcast.10), kind=kOutput, calls=%fused_computation.4 | convolution fusion | flops 6979321856 | bytes 18612224 | tf_op jit(solution)/shard_map/dot_general | solution.py:30
  711.8 0.0 reduce-scatter.5.cloned.1.call-start
  711.9 88.4 %reduce-scatter.3.cloned.1.call-done = f32[1024,256]{0,1:T(8,128)} async-done(((f32[1024,2048]{0,1:T(8,128)}), f32[1024,256]{0,1:T(8,128)}) %reduce-scatter.3.cloned.1.call-update) | async-done | bytes 1048592 | tf_op jit(solution)/shard_map/reduce_scatter | solution.py:31
  800.2 29.2 %reduce-scatter.5.cloned.1.call-done = f32[256,256]{0,1:T(8,128)} async-done(((f32[1024,256]{0,1:T(8,128)}), f32[256,256]{0,1:T(8,128)}) %reduce-scatter.5.cloned.1.call-update) | async-done | bytes 262160 | tf_op jit(solution)/shard_map/reduce_scatter | solution.py:32
  829.4 1.8 copy.17
  (18 shorter events, 0.1 us)
Async XLA Ops:
  6.5 320.7 %copy-start = (f32[1664,256]{1,0:T(8,128)S(1)}, f32[1664,256]{1,0:T(8,128)}, u32[]{:S(2)}) copy-start(f32[1664,256]{1,0:T(8,128)} %param.11) | copy-start | bytes 5111812
  20.4 302.7 %all-to-all-start = ((f32[8,1664,256]{1,2,0:T(8,128)}), f32[8,1664,256]{1,2,0:T(8,128)}, u32[]{:S(2)}, u32[]{:S(2)}) async-start(f32[8,1664,256]{1,2,0:T(8,128)} %copy.15), calls=%async_computation | async-start | bytes 27262976 | tf_op jit(solution)/shard_map/all_to_all | solution.py:23
  323.0 375.8 %all-to-all-start.1 = ((bf16[32,32,1664]{2,0,1:T(8,128)(2,1)}), bf16[32,32,1664]{2,0,1:T(8,128)(2,1)}, u32[]{:S(2)}, u32[]{:S(2)}) async-start(bf16[32,32,1664]{2,0,1:T(8,128)(2,1)} %bitcast.40), calls=%async_computation.1 | async-start | bytes 6815744 | tf_op jit(solution)/shard_map/all_to_all | solution.py:29
  327.2 178.0 %all-reduce.3.cloned.1.call-start = ((), (), s32[]{:S(2)}) async-start(), calls=%async_computation.4 | async-start | bytes 4194304 | tf_op jit(solution)/shard_map/psum | solution.py:25
  353.1 152.1 %copy-start.4 = (f32[256,256]{1,0:T(8,128)S(1)}, f32[256,256]{1,0:T(8,128)}, u32[]{:S(2)}) copy-start(f32[256,256]{1,0:T(8,128)} %param.13) | copy-start | bytes 786436
  353.1 325.8 %all-reduce.5.cloned.1.call-start = ((), (), s32[]{:S(2)}) async-start(), calls=%async_computation.5 | async-start | bytes 4194304 | tf_op jit(solution)/shard_map/psum | solution.py:25
  510.3 21.8 %copy-start.3 = (f32[1664,256]{1,0:T(8,128)S(1)}, f32[1664,256]{1,0:T(8,128)}, u32[]{:S(2)}) copy-start(f32[1664,256]{1,0:T(8,128)} %param.10) | copy-start | bytes 5111812
  527.2 4.9 copy-start.2
  545.3 0.7 copy-start.6
  545.3 133.6 %copy-start.5 = (f32[256,256]{1,0:T(8,128)S(1)}, f32[256,256]{1,0:T(8,128)}, u32[]{:S(2)}) copy-start(f32[256,256]{1,0:T(8,128)} %param.12) | copy-start | bytes 786436
  545.3 254.9 %reduce-scatter.3.cloned.1.call-start = ((), (), s32[]{:S(2)}) async-start(), calls=%async_computation.6 | async-start | bytes 9437184 | tf_op jit(solution)/shard_map/reduce_scatter | solution.py:31
  711.8 119.4 %copy-start.1 = (f32[1664,256]{1,0:T(8,128)S(1)}, f32[1664,256]{1,0:T(8,128)}, u32[]{:S(2)}) copy-start(f32[1664,256]{1,0:T(8,128)} %param.11) | copy-start | bytes 5111812
  711.8 117.6 %reduce-scatter.5.cloned.1.call-start = ((), (), s32[]{:S(2)}) async-start(), calls=%async_computation.7 | async-start | bytes 1310720 | tf_op jit(solution)/shard_map/reduce_scatter | solution.py:32
Sparse Core Ops, SparseCore 0:
  353.2 151.8 all-reduce.2
  545.4 133.4 all-reduce.4
  711.9 88.2 reduce-scatter.2
  803.0 26.4 reduce-scatter.4
where the time goes:
time: 838 us
  waiting for transfers between devices  684 us (82%)
  matrix products  93.9 us (11%)
  local copies, waits for them, and re-layouts  25.3 us (3%)
  between operations  13.2 us (2%)
  starting transfers between devices  10.8 us (1%)
  blocking collectives  10.6 us (1%)
    all_to_all x1, waiting for transfers between devices, per_device(): lax.all_to_all(eigvecs, 'col', split_axis=0, concat_axis=1, tiled=True)  292 us
    psum x2, waiting for transfers between devices, per_device(): inner = lax.psum(partial_inner(panel, block), ('row', 'col'))  274 us
    reduce_scatter x1, waiting for transfers between devices, per_device(): lax.psum_scatter(partial_value, 'col', scatter_dimension=1, tiled=True)  88.4 us
    dot_general x2, matrix products, partial_inner(): jnp.dot(panel.T, block, precision=lax.Precision.HIGHEST, preferred_elemen...  39 us
    dot_general x2, matrix products, local_update(): jnp.dot(panel, middle, precision=lax.Precision.HIGHEST, preferred_element...  33.3 us
    reduce_scatter x1, waiting for transfers between devices, per_device(): summed = lax.psum_scatter(by_column, 'row', scatter_dimension=0, tiled=True)  29.2 us
  transfers between devices with their start and end apart: 6, of which 5 were waited for; matrix products, arithmetic and copies ran while one was open for 10% of the time, Pallas kernels for 0%

commit v1 on v0

--- a/solution.py
+++ b/solution.py
@@ -22,7 +22,7 @@
 def per_device(tokens, eigvecs, eigvals, v_first, v_second, t_first, t_second):
     block = lax.all_to_all(eigvecs, "col", split_axis=0, concat_axis=1, tiled=True)
     for panel, factor in ((v_second, t_second), (v_first, t_first)):
-        inner = lax.psum(partial_inner(panel, block), ("row", "col"))
+        inner = lax.psum(lax.psum(partial_inner(panel, block), "row"), "col")
         block = local_update(block, panel, factor, inner)
     every_value = lax.all_gather(eigvals, "col", axis=0, tiled=True)
     whitening = (block * lax.rsqrt(every_value)[None, :]).astype(jnp.bfloat16)

time: 838 us -> 891 us (1.063); the launches traced: 838 us -> 881 us
  blocking collectives: 10.6 us -> 315 us
  waiting for transfers between devices: 684 us -> 426 us
    all_to_all x0 -> x1, blocking collectives: none -> 303 us  [per_device(): lax.all_to_all(eigvecs, 'col', split_axis=0, concat_axis=1, tiled=True)]
    all_to_all x1 -> x0, waiting for transfers between devices: 292 us -> none  [per_device(): lax.all_to_all(eigvecs, 'col', split_axis=0, concat_axis=1, tiled=True)]
    psum x2 -> x4, waiting for transfers between devices: 274 us -> 308 us  [per_device(): inner = lax.psum(lax.psum(partial_inner(panel, block), 'row'), 'col')]
  transfers between devices with their start and end apart: 6 -> 7, of which waited for: 5 -> 6; matrix products, arithmetic and copies ran while one was open for 10% -> 7% of each run, Pallas kernels for 0% -> 0%
where the time goes in v1:
time: 891 us; the launch traced here: 881 us
  waiting for transfers between devices  426 us (48%)
  blocking collectives  315 us (35%)
  matrix products  91.7 us (10%)
  local copies, waits for them, and re-layouts  29.5 us (3%)
  between operations  14 us (2%)
    psum x4, waiting for transfers between devices, per_device(): inner = lax.psum(lax.psum(partial_inner(panel, block), 'row'), 'col')  308 us
    all_to_all x1, blocking collectives, per_device(): lax.all_to_all(eigvecs, 'col', split_axis=0, concat_axis=1, tiled=True)  303 us
    reduce_scatter x1, waiting for transfers between devices, per_device(): lax.psum_scatter(partial_value, 'col', scatter_dimension=1, tiled=True)  89.2 us
    dot_general x2, matrix products, partial_inner(): jnp.dot(panel.T, block, precision=lax.Precision.HIGHEST, preferred_elemen...  36.5 us
    dot_general x2, matrix products, local_update(): jnp.dot(panel, middle, precision=lax.Precision.HIGHEST, preferred_element...  33.5 us
    reduce_scatter x1, waiting for transfers between devices, per_device(): summed = lax.psum_scatter(by_column, 'row', scatter_dimension=0, tiled=True)  29.2 us
  transfers between devices with their start and end apart: 7, of which 6 were waited for; matrix products, arithmetic and copies ran while one was open for 7% of the time, Pallas kernels for 0%

profile of v1, /device:TPU:0, one launch (start us, length us, event | category | flops | bytes accessed | tf_op | source)
XLA Modules:
  0.0 881.1 jit_solution(1540341761491862977)
XLA Ops:
  6.5 13.9 %copy.15 = f32[8,1664,256]{1,2,0:T(8,128)} copy(f32[8,1664,256]{2,1,0:T(8,128)} %bitcast.41) | data formatting | bytes 27262976 | tf_op jit(solution)/shard_map/all_to_all | solution.py:23
  20.4 302.6 %all_to_all.38 = f32[8,1664,256]{1,2,0:T(8,128)S(1)} all-to-all(f32[8,1664,256]{1,2,0:T(8,128)} %copy.15), channel_id=1, replica_groups=mesh['row'=4,'col'=8] {'col'}, dimensions={0} | all-to-all | bytes 27262976 | tf_op jit(solution)/shard_map/all_to_all | solution.py:23
  323.0 4.9 copy-done.3
  327.9 23.4 %fusion.2 = f32[256,2048]{1,0:T(8,128)} fusion(f32[1664,256]{1,0:T(8,128)S(1)} %copy-done, f32[1664,2048]{0,1:T(8,128)S(1)} %bitcast.39), kind=kOutput, calls=%fused_computation.7 | convolution fusion | flops 10468982784 | bytes 17432576 | tf_op jit(solution)/shard_map/dot_general | solution.py:17
  351.3 0.0 all-reduce.7.cloned.1.call-start
  351.4 68.5 %all-reduce.5.cloned.1.call-done = f32[256,2048]{1,0:T(8,128)} async-done(((f32[256,2048]{1,0:T(8,128)}), f32[256,2048]{1,0:T(8,128)}) %all-reduce.5.cloned.1.call-update) | async-done | bytes 2097168 | tf_op jit(solution)/shard_map/psum | solution.py:25
  419.9 4.0 copy.20
  423.9 4.7 all-to-all-start.1
  428.7 0.0 all-reduce.9.cloned.1.call-start
  428.7 115.5 %all-reduce.7.cloned.1.call-done = f32[256,2048]{1,0:T(8,128)} async-done(((f32[256,2048]{1,0:T(8,128)}), f32[256,2048]{1,0:T(8,128)}) %all-reduce.7.cloned.1.call-update) | async-done | bytes 2097168 | tf_op jit(solution)/shard_map/psum | solution.py:25
  544.2 5.2 fusion.3
  549.4 17.1 %bitcast_subtract_fusion.1 = f32[1664,2048]{0,1:T(8,128)S(1)} fusion(f32[1664,2048]{0,1:T(8,128)} %bitcast.40, f32[2048,256]{1,0:T(8,128)S(1)} %fusion.3, f32[1664,256]{1,0:T(8,128)S(1)} %copy-done), kind=kOutput, calls=%fused_computation.3 | convolution fusion | flops 10472390656 | bytes 31064064 | tf_op jit(solution)/shard_map/dot_general | solution.py:11
  566.5 4.9 copy-done.2
  571.4 13.1 %convolution_bitcast_fusion.1 = f32[256,2048]{0,1:T(8,128)} fusion(f32[1664,2048]{0,1:T(8,128)S(1)} %bitcast_subtract_fusion.1, f32[1664,256]{1,0:T(8,128)S(1)} %copy-done.4), kind=kOutput, calls=%fused_computation.6 | convolution fusion | flops 10468982784 | bytes 17432576 | tf_op jit(solution)/shard_map/dot_general | solution.py:17
  584.6 68.7 %all-reduce.9.cloned.1.call-done = f32[256,2048]{0,1:T(8,128)} async-done(((f32[256,2048]{0,1:T(8,128)}), f32[256,2048]{0,1:T(8,128)}) %all-reduce.9.cloned.1.call-update) | async-done | bytes 2097168 | tf_op jit(solution)/shard_map/psum | solution.py:25
  653.3 12.0 %all-gather = f32[8,1,256]{2,1,0:T(1,128)S(1)} all-gather(f32[1,1,256]{2,1,0:T(1,128)S(1)} %bitcast.45), channel_id=1, replica_groups=mesh['row'=4,'col'=8] {'col'}, dimensions={0}, use_global_device_ids=true | all-gather | bytes 9216 | tf_op jit(solution)/shard_map/all_gather | solution.py:27
  665.4 55.3 %all-reduce.11.cloned.1.call-done = f32[256,2048]{0,1:T(8,128)} async-done(((f32[256,2048]{0,1:T(8,128)}), f32[256,2048]{0,1:T(8,128)}) %all-reduce.11.cloned.1.call-update) | async-done | bytes 2097168 | tf_op jit(solution)/shard_map/psum | solution.py:25
  720.6 3.5 fusion.4
  724.1 16.4 %fusion.1 = bf16[1664,2048]{0,1:T(8,128)(2,1)} fusion(f32[1664,2048]{0,1:T(8,128)} %copy-done.2, f32[2048,256]{1,0:T(8,128)S(1)} %fusion.4, f32[1664,256]{1,0:T(8,128)S(1)} %copy-done.4, f32[2048]{0:T(1024)S(1)} %bitcast.44), kind=kOutput, calls=%fused_computation.2 | convolution fusion | flops 10479206400 | bytes 24256512 | tf_op jit(solution)/shard_map/dot_general | solution.py:11
  740.6 12.9 %convolution_bitcast_fusion = f32[1024,2048]{0,1:T(8,128)} fusion(bf16[1664,2048]{0,1:T(8,128)(2,1)} %fusion.1, bf16[1024,1664]{1,0:T(8,128)(2,1)} %bitcast.10), kind=kOutput, calls=%fused_computation.4 | convolution fusion | flops 6979321856 | bytes 18612224 | tf_op jit(solution)/shard_map/dot_general | solution.py:30
  753.5 0.0 reduce-scatter.5.cloned.1.call-start
  753.6 89.2 %reduce-scatter.3.cloned.1.call-done = f32[1024,256]{0,1:T(8,128)} async-done(((f32[1024,2048]{0,1:T(8,128)}), f32[1024,256]{0,1:T(8,128)}) %reduce-scatter.3.cloned.1.call-update) | async-done | bytes 1048592 | tf_op jit(solution)/shard_map/reduce_scatter | solution.py:31
  842.9 29.2 %reduce-scatter.5.cloned.1.call-done = f32[256,256]{0,1:T(8,128)} async-done(((f32[1024,256]{0,1:T(8,128)}), f32[256,256]{0,1:T(8,128)}) %reduce-scatter.5.cloned.1.call-update) | async-done | bytes 262160 | tf_op jit(solution)/shard_map/reduce_scatter | solution.py:32
  872.0 1.8 copy.17
  (25 shorter events, 0.2 us)
Async XLA Ops:
  6.5 321.3 %copy-start = (f32[1664,256]{1,0:T(8,128)S(1)}, f32[1664,256]{1,0:T(8,128)}, u32[]{:S(2)}) copy-start(f32[1664,256]{1,0:T(8,128)} %param.11) | copy-start | bytes 5111812
  6.5 413.4 %all-reduce.5.cloned.1.call-start = ((), (), s32[]{:S(2)}) async-start(), calls=%async_computation.4 | async-start | bytes 4194304 | tf_op jit(solution)/shard_map/psum | solution.py:25
  323.0 4.9 copy-start.3
  351.3 192.9 %all-reduce.7.cloned.1.call-start = ((), (), s32[]{:S(2)}) async-start(), calls=%async_computation.5 | async-start | bytes 4194304 | tf_op jit(solution)/shard_map/psum | solution.py:25
  423.9 120.3 %copy-start.5 = (f32[256,256]{1,0:T(8,128)S(1)}, f32[256,256]{1,0:T(8,128)}, u32[]{:S(2)}) copy-start(f32[256,256]{1,0:T(8,128)} %param.13) | copy-start | bytes 786436
  423.9 316.6 %all-to-all-start.1 = ((bf16[32,32,1664]{2,0,1:T(8,128)(2,1)}), bf16[32,32,1664]{2,0,1:T(8,128)(2,1)}, u32[]{:S(2)}, u32[]{:S(2)}) async-start(bf16[32,32,1664]{2,0,1:T(8,128)(2,1)} %bitcast.42), calls=%async_computation.1 | async-start | bytes 6815744 | tf_op jit(solution)/shard_map/all_to_all | solution.py:29
  428.7 224.6 %all-reduce.9.cloned.1.call-start = ((), (), s32[]{:S(2)}) async-start(), calls=%async_computation.6 | async-start | bytes 4194304 | tf_op jit(solution)/shard_map/psum | solution.py:25
  549.4 22.0 %copy-start.4 = (f32[1664,256]{1,0:T(8,128)S(1)}, f32[1664,256]{1,0:T(8,128)}, u32[]{:S(2)}) copy-start(f32[1664,256]{1,0:T(8,128)} %param.10) | copy-start | bytes 5111812
  566.5 4.9 copy-start.2
  584.5 68.8 %copy-start.7 = (f32[256]{0:T(256)S(1)}, f32[256]{0:T(256)}, u32[]{:S(2)}) copy-start(f32[256]{0:T(256)} %param.9) | copy-start | bytes 3076
  584.5 136.1 %copy-start.6 = (f32[256,256]{1,0:T(8,128)S(1)}, f32[256,256]{1,0:T(8,128)}, u32[]{:S(2)}) copy-start(f32[256,256]{1,0:T(8,128)} %param.12) | copy-start | bytes 786436
  584.6 136.1 %all-reduce.11.cloned.1.call-start = ((), (), s32[]{:S(2)}) async-start(), calls=%async_computation.7 | async-start | bytes 4194304 | tf_op jit(solution)/shard_map/psum | solution.py:25
  653.3 189.5 %reduce-scatter.3.cloned.1.call-start = ((), (), s32[]{:S(2)}) async-start(), calls=%async_computation.8 | async-start | bytes 9437184 | tf_op jit(solution)/shard_map/reduce_scatter | solution.py:31
  753.5 120.3 %copy-start.1 = (f32[1664,256]{1,0:T(8,128)S(1)}, f32[1664,256]{1,0:T(8,128)}, u32[]{:S(2)}) copy-start(f32[1664,256]{1,0:T(8,128)} %param.11) | copy-start | bytes 5111812
  753.5 118.5 %reduce-scatter.5.cloned.1.call-start = ((), (), s32[]{:S(2)}) async-start(), calls=%async_computation.9 | async-start | bytes 1310720 | tf_op jit(solution)/shard_map/reduce_scatter | solution.py:32
Sparse Core Ops, SparseCore 0:
  351.4 68.4 all-reduce.4
  422.3 121.9 all-reduce.6
  584.7 68.5 all-reduce.8
  655.5 65.0 all-reduce.10
  753.7 89.1 reduce-scatter.2
  845.6 26.4 reduce-scatter.4
